TPU v7x, 32 devices: a whole 2x2x4 slice. The times are simulated.
32 devices in a mesh: row: 2 (over y), col: 16 (over z, x, core).
Axes of the slice: x: 2, y: 2, z: 4, core: 2. Of those that a mesh axis runs over, the one named last changes fastest.
Arguments:
- w_slab: float32 [512, 16384], P('row', 'col'), may hold values from -0.25 to 0.25
- prior_cov: float32 [16384, 16384], P('row', 'col'), as said below
Outputs:
- posterior: float32 [16384, 16384], P('row', 'col')
Inputs may be any that keep to these rules, and one draw needn't show every extreme that they name: prior_cov is symmetric.
All inputs are finite; a program needn't handle non-finite values.
Results may differ from a plain program's by a relative error of at most 0.00005.
Values sent between devices are 32-bit elements; how exact they have to be, the bound alone decides.
No kernel may reach another device: no remote copies, remote signals or barrier semaphores. Data moves between devices by JAX's collectives and lax.ppermute only.
A program may use at most 256 MiB of HBM per device.

v0:
```python
import jax
import jax.numpy as jnp
from jax import lax
from jax.sharding import PartitionSpec as P


def from_root(value, axis, source):
    kept = jnp.where(lax.axis_index(axis) == source, value, 0).astype(value.dtype)
    return lax.psum(kept, axis)


def shards(w_slab, prior_cov):
    own_block = lax.all_gather(w_slab, "row", axis=0, tiled=True)
    width = own_block.shape[1]
    groups = lax.axis_size("col") // lax.axis_size("row")
    row_index = lax.axis_index("row")
    result = prior_cov
    for step in range(groups):
        slot = jnp.int32(step)
        root = row_index * groups + slot
        received = from_root(own_block, "col", root)
        product = lax.dot_general(
            received,
            own_block,
            (((0,), (0,)), ((), ())),
            precision=lax.Precision.HIGHEST,
            preferred_element_type=jnp.float32,
        )
        start = slot * width
        current = lax.dynamic_slice_in_dim(result, start, width, 0)
        result = lax.dynamic_update_slice_in_dim(result, current - product, start, 0)
    return result


def solution(mesh):
    return jax.shard_map(
        shards,
        mesh=mesh,
        in_specs=(P("row", "col"), P("row", "col")),
        out_specs=P("row", "col"),
        check_vma=False,
    )
```

profile of v0, /device:TPU:0, one launch (start us, length us, event | category | flops | bytes accessed | tf_op | source)
XLA Modules:
  0.0 460.4 jit_solution(723718083218252764)
XLA Ops:
  6.5 0.0 all-gather.2.cloned.1.call-start
  6.5 23.5 %copy.20 = f32[8192,1024]{1,0:T(8,128)} copy(f32[8192,1024]{1,0:T(8,128)} %param.3) | data formatting | bytes 67108864
  30.0 0.0 all-gather.2.cloned.1.call-update
  30.0 0.0 all-reduce.3.cloned.1.call-start
  30.1 35.9 %all-gather.2.cloned.1.call-done = f32[512,1024]{1,0:T(8,128)} async-done(((f32[256,1024]{1,0:T(8,128)}), f32[512,1024]{1,0:T(8,128)}) %all-gather.2.cloned.1.call-update) | async-done | bytes 2097168 | tf_op jit(solution)/shard_map/all_gather | solution.py:13
  66.0 7.8 %broadcast_select_fusion = (f32[512,1024]{1,0:T(8,128)}, f32[512,1024]{1,0:T(8,128)}, f32[512,1024]{1,0:T(8,128)}, f32[512,1024]{1,0:T(8,128)}, f32[512,1024]{1,...) fusion(f32[512,1024]{1,0:T(8,128)} %all-gather.2.cloned.1.call-done, pred[]{:T(512)S(6)} %eq.31, ...), kind=kLoop, calls=%fused_computation.15 | loop fusion | flops 4194304 | bytes 18874376 | tf_op jit(solution)/shard_map/jit(_where)/select_n | solution.py:8
  73.8 0.0 copy-start
  73.8 0.0 all-reduce.3.cloned.1.call-update
  73.9 298.4 %all-reduce.3.cloned.1.call-done = (f32[512,1024]{1,0:T(8,128)}, f32[512,1024]{1,0:T(8,128)}, f32[512,1024]{1,0:T(8,128)}, f32[512,1024]{1,0:T(8,128)}, f32[512,...) async-done(((f32[512,1024]{1,0:T(8,128)}, f32[512,1024]{1,0:T(8,128)}, f32[512,1024]{1,0:T(8,128)}, f32[512,1024]{1,0:T(8,128)}, ...) | async-done | bytes 16777232 | tf_op jit(solution)/shard_map/psum | solution.py:9
  372.3 0.0 copy-done
  372.3 0.0 copy-start.7
  372.3 10.4 %subtract_dynamic-update-slice_fusion = f32[8192,1024]{1,0:T(8,128)} fusion(f32[8192,1024]{1,0:T(8,128)} %copy.20, f32[512,1024]{1,0:T(8,128)} %get-tuple-element.5, f32[512,1024]{1,0:T(8,128)S(1)} %copy-done), kind=kOutput, calls=%fused_computation.14 | convolution fusion | flops 6443499520 | bytes 12582912 | tf_op jit(solution)/shard_map/dot_general | solution.py:22
  382.7 0.0 copy-done.7
  382.7 0.0 copy-start.6
  382.7 10.1 %fusion.6 = f32[8192,1024]{1,0:T(8,128)} fusion(f32[8192,1024]{1,0:T(8,128)} %subtract_dynamic-update-slice_fusion, f32[512,1024]{1,0:T(8,128)S(1)} %copy-done.7, f32[512,1024]{1,0:T(8,128)S(1)} %copy-done), kind=kOutput, calls=%fused_computation.13 | convolution fusion | flops 6443499520 | bytes 12582912 | tf_op jit(solution)/shard_map/dot_general | solution.py:22
  392.8 0.0 copy-done.6
  392.8 0.0 copy-start.5
  392.8 10.1 %fusion.5 = f32[8192,1024]{1,0:T(8,128)} fusion(f32[8192,1024]{1,0:T(8,128)} %fusion.6, f32[512,1024]{1,0:T(8,128)S(1)} %copy-done.6, f32[512,1024]{1,0:T(8,128)S(1)} %copy-done), kind=kOutput, calls=%fused_computation.11 | convolution fusion | flops 6443499520 | bytes 12582912 | tf_op jit(solution)/shard_map/dot_general | solution.py:22
  402.9 0.0 copy-done.5
  402.9 0.0 copy-start.4
  402.9 10.2 %fusion.4 = f32[8192,1024]{1,0:T(8,128)} fusion(f32[8192,1024]{1,0:T(8,128)} %fusion.5, f32[512,1024]{1,0:T(8,128)S(1)} %copy-done.5, f32[512,1024]{1,0:T(8,128)S(1)} %copy-done), kind=kOutput, calls=%fused_computation.9 | convolution fusion | flops 6443499520 | bytes 12582912 | tf_op jit(solution)/shard_map/dot_general | solution.py:22
  413.1 0.0 copy-done.4
  413.1 0.0 copy-start.3
  413.1 10.1 %fusion.3 = f32[8192,1024]{1,0:T(8,128)} fusion(f32[8192,1024]{1,0:T(8,128)} %fusion.4, f32[512,1024]{1,0:T(8,128)S(1)} %copy-done.4, f32[512,1024]{1,0:T(8,128)S(1)} %copy-done), kind=kOutput, calls=%fused_computation.7 | convolution fusion | flops 6443499520 | bytes 12582912 | tf_op jit(solution)/shard_map/dot_general | solution.py:22
  423.2 0.0 copy-done.3
  423.2 0.0 copy-start.2
  423.2 10.1 %fusion.2 = f32[8192,1024]{1,0:T(8,128)} fusion(f32[8192,1024]{1,0:T(8,128)} %fusion.3, f32[512,1024]{1,0:T(8,128)S(1)} %copy-done.3, f32[512,1024]{1,0:T(8,128)S(1)} %copy-done), kind=kOutput, calls=%fused_computation.5 | convolution fusion | flops 6443499520 | bytes 12582912 | tf_op jit(solution)/shard_map/dot_general | solution.py:22
  433.3 0.0 copy-done.2
  433.3 0.0 copy-start.1
  433.3 10.3 %fusion.1 = f32[8192,1024]{1,0:T(8,128)} fusion(f32[8192,1024]{1,0:T(8,128)} %fusion.2, f32[512,1024]{1,0:T(8,128)S(1)} %copy-done.2, f32[512,1024]{1,0:T(8,128)S(1)} %copy-done), kind=kOutput, calls=%fused_computation.3 | convolution fusion | flops 6443499520 | bytes 12582912 | tf_op jit(solution)/shard_map/dot_general | solution.py:22
  443.6 0.0 copy-done.1
  443.6 9.9 %fusion = f32[8192,1024]{1,0:T(8,128)} fusion(f32[8192,1024]{1,0:T(8,128)} %fusion.1, f32[512,1024]{1,0:T(8,128)S(1)} %copy-done.1, f32[512,1024]{1,0:T(8,128)S(1)} %copy-done), kind=kOutput, calls=%fused_computation.1 | convolution fusion | flops 6443499520 | bytes 12582912 | tf_op jit(solution)/shard_map/dot_general | solution.py:22
Async XLA Ops:
  6.5 59.5 %all-gather.2.cloned.1.call-start = ((), (), s32[]{:S(2)}) async-start(), calls=%async_computation | async-start | bytes 3145728 | tf_op jit(solution)/shard_map/all_gather | solution.py:13
  30.0 342.3 %all-reduce.3.cloned.1.call-start = ((), (), s32[]{:S(2)}) async-start(), calls=%async_computation.1 | async-start | bytes 33554432 | tf_op jit(solution)/shard_map/psum | solution.py:9
  73.8 298.5 %copy-start = (f32[512,1024]{1,0:T(8,128)S(1)}, f32[512,1024]{1,0:T(8,128)}, u32[]{:S(2)}) copy-start(f32[512,1024]{1,0:T(8,128)} %all-gather.2.cloned.1.call-done) | copy-start | bytes 6291460
  372.3 10.4 %copy-start.7 = (f32[512,1024]{1,0:T(8,128)S(1)}, f32[512,1024]{1,0:T(8,128)}, u32[]{:S(2)}) copy-start(f32[512,1024]{1,0:T(8,128)} %get-tuple-element.6) | copy-start | bytes 6291460
  382.7 10.1 %copy-start.6 = (f32[512,1024]{1,0:T(8,128)S(1)}, f32[512,1024]{1,0:T(8,128)}, u32[]{:S(2)}) copy-start(f32[512,1024]{1,0:T(8,128)} %get-tuple-element.7) | copy-start | bytes 6291460
  392.8 10.1 %copy-start.5 = (f32[512,1024]{1,0:T(8,128)S(1)}, f32[512,1024]{1,0:T(8,128)}, u32[]{:S(2)}) copy-start(f32[512,1024]{1,0:T(8,128)} %get-tuple-element.8) | copy-start | bytes 6291460
  402.9 10.2 %copy-start.4 = (f32[512,1024]{1,0:T(8,128)S(1)}, f32[512,1024]{1,0:T(8,128)}, u32[]{:S(2)}) copy-start(f32[512,1024]{1,0:T(8,128)} %get-tuple-element.9) | copy-start | bytes 6291460
  413.1 10.1 %copy-start.3 = (f32[512,1024]{1,0:T(8,128)S(1)}, f32[512,1024]{1,0:T(8,128)}, u32[]{:S(2)}) copy-start(f32[512,1024]{1,0:T(8,128)} %get-tuple-element.10) | copy-start | bytes 6291460
  423.2 10.1 %copy-start.2 = (f32[512,1024]{1,0:T(8,128)S(1)}, f32[512,1024]{1,0:T(8,128)}, u32[]{:S(2)}) copy-start(f32[512,1024]{1,0:T(8,128)} %get-tuple-element.11) | copy-start | bytes 6291460
  433.3 10.3 %copy-start.1 = (f32[512,1024]{1,0:T(8,128)S(1)}, f32[512,1024]{1,0:T(8,128)}, u32[]{:S(2)}) copy-start(f32[512,1024]{1,0:T(8,128)} %get-tuple-element.12) | copy-start | bytes 6291460
Sparse Core Ops, SparseCore 0:
  30.1 35.8 all-gather.1
  74.0 298.2 all-reduce.2
where the time goes:
time: 461 us; the launch traced here: 460 us
  waiting for transfers between devices  334 us (72%)
  matrix products  81.2 us (18%)
  local copies, waits for them, and re-layouts  23.5 us (5%)
  between operations  13.4 us (3%)
  other arithmetic  7.85 us (2%)
    psum x1, waiting for transfers between devices, from_root(): return lax.psum(kept, axis)  298 us
    dot_general x8, matrix products, shards(): lax.dot_general(received, own_block, (((0,), (0,)), ((), ())), precision=...  81.2 us
    all_gather x1, waiting for transfers between devices, shards(): own_block = lax.all_gather(w_slab, 'row', axis=0, tiled=True)  35.9 us
    unnamed x17, local copies, waits for them, and re-layouts  23.5 us
  transfers between devices with their start and end apart: 2, of which 2 were waited for; matrix products, arithmetic and copies ran while one was open for 0% of the time, Pallas kernels for 0%

commit v1 on v0

--- a/solution.py
+++ b/solution.py
@@ -10,7 +10,14 @@
 
 
 def shards(w_slab, prior_cov):
-    own_block = lax.all_gather(w_slab, "row", axis=0, tiled=True)
+    ways, here, step_2 = (lax.axis_size("row"), lax.axis_index("row"), w_slab.shape[0])
+    line, have = (w_slab, 1)
+    while have < ways:
+        line = jnp.concatenate(
+            [line, lax.ppermute(line, "row", [(d, (d - have) % ways) for d in range(ways)])], axis=0
+        )
+        have = 2 * have
+    own_block = jnp.roll(line, here * step_2, axis=0)
     width = own_block.shape[1]
     groups = lax.axis_size("col") // lax.axis_size("row")
     row_index = lax.axis_index("row")

time: 461 us -> 454 us (0.985)
  waiting for transfers between devices: 334 us -> 323 us
    all_gather x1 -> x0, waiting for transfers between devices: 35.9 us -> none  [shards(): own_block = lax.all_gather(w_slab, 'row', axis=0, tiled=True)]
    ppermute x0 -> x1, waiting for transfers between devices: none -> 23.3 us  [shards(): lax.ppermute(line, 'row', [(d, (d - have) % ways) for d in range(ways)])]
    select_n x1 -> x2, other arithmetic: 7.85 us -> 9.35 us  [from_root(): jnp.where(lax.axis_index(axis) == source, value, 0).astype(value.dtype)]
where the time goes in v1:
time: 454 us
  waiting for transfers between devices  323 us (71%)
  matrix products  81.2 us (18%)
  local copies, waits for them, and re-layouts  23.6 us (5%)
  between operations  13.4 us (3%)
  other arithmetic  9.35 us (2%)
    psum x1, waiting for transfers between devices, from_root(): return lax.psum(kept, axis)  300 us
    dot_general x8, matrix products, shards(): lax.dot_general(received, own_block, (((0,), (0,)), ((), ())), precision=...  81.2 us
    unnamed x17, local copies, waits for them, and re-layouts  23.6 us
    ppermute x1, waiting for transfers between devices, shards(): lax.ppermute(line, 'row', [(d, (d - have) % ways) for d in range(ways)])  23.3 us
    select_n x2, other arithmetic, from_root(): jnp.where(lax.axis_index(axis) == source, value, 0).astype(value.dtype)  9.35 us
  transfers between devices with their start and end apart: 2, of which 2 were waited for; matrix products, arithmetic and copies ran while one was open for 0% of the time, Pallas kernels for 0%

profile of v1, /device:TPU:0, one launch (start us, length us, event | category | flops | bytes accessed | tf_op | source)
XLA Modules:
  0.0 453.7 jit_solution(9018871552728309801)
XLA Ops:
  6.5 0.0 copy-start.7
  6.5 0.0 all-reduce.3.cloned.1.call-start
  6.5 23.5 %copy.20 = f32[8192,1024]{1,0:T(8,128)} copy(f32[8192,1024]{1,0:T(8,128)} %param.3) | data formatting | bytes 67108864
  30.1 0.0 copy-done.7
  30.1 3.0 collective-permute-start
  33.1 23.3 %collective-permute-done = f32[256,1024]{1,0:T(8,128)} collective-permute-done((f32[256,1024]{1,0:T(8,128)S(1)}, f32[256,1024]{1,0:T(8,128)}, u32[]{:S(2)}, u32[]{:S(2)}) %collective-permute-start) | collective-permute-done | bytes 1048608 | tf_op jit(solution)/shard_map/ppermute | solution.py:17
  56.3 4.0 broadcast_select_fusion
  60.3 5.4 %broadcast_select_fusion.1 = (f32[512,1024]{1,0:T(8,128)}, f32[512,1024]{1,0:T(8,128)}, f32[512,1024]{1,0:T(8,128)}, f32[512,1024]{1,0:T(8,128)}, f32[512,1024]{...) fusion(f32[512,1024]{1,0:T(8,128)S(1)} %get-tuple-element.14, pred[]{:T(512)S(6)} %eq.33, pred[]{:T(512)S(6)} %eq.32, ...), kind=kLoop, calls=%fused_computation.23 | loop fusion | flops 3670016 | bytes 16777224 | tf_op jit(solution)/shard_map/jit(_where)/select_n | solution.py:8
  65.7 0.0 all-reduce.3.cloned.1.call-update
  65.7 299.9 %all-reduce.3.cloned.1.call-done = (f32[512,1024]{1,0:T(8,128)}, f32[512,1024]{1,0:T(8,128)}, f32[512,1024]{1,0:T(8,128)}, f32[512,1024]{1,0:T(8,128)}, f32[512,...) async-done(((f32[512,1024]{1,0:T(8,128)}, f32[512,1024]{1,0:T(8,128)}, f32[512,1024]{1,0:T(8,128)}, f32[512,1024]{1,0:T(8,128)}, ...) | async-done | bytes 16777232 | tf_op jit(solution)/shard_map/psum | solution.py:9
  365.6 0.0 copy-start.6
  365.6 10.4 %subtract_dynamic-update-slice_fusion = f32[8192,1024]{1,0:T(8,128)} fusion(f32[8192,1024]{1,0:T(8,128)} %copy.20, f32[512,1024]{1,0:T(8,128)} %get-tuple-element.5, f32[512,1024]{1,0:T(8,128)S(1)} %get-tuple-element.14), kind=kOutput, calls=%fused_computation.18 | convolution fusion | flops 6443499520 | bytes 12582912 | tf_op jit(solution)/shard_map/dot_general | solution.py:29
  376.0 0.0 copy-done.6
  376.0 0.0 copy-start.5
  376.0 10.1 %fusion.6 = f32[8192,1024]{1,0:T(8,128)} fusion(f32[8192,1024]{1,0:T(8,128)} %subtract_dynamic-update-slice_fusion, f32[512,1024]{1,0:T(8,128)S(1)} %copy-done.6, f32[512,1024]{1,0:T(8,128)S(1)} %get-tuple-element.14), kind=kOutput, calls=%fused_computation.13 | convolution fusion | flops 6443499520 | bytes 12582912 | tf_op jit(solution)/shard_map/dot_general | solution.py:29
  386.1 0.0 copy-done.5
  386.1 0.0 copy-start.4
  386.1 10.2 %fusion.5 = f32[8192,1024]{1,0:T(8,128)} fusion(f32[8192,1024]{1,0:T(8,128)} %fusion.6, f32[512,1024]{1,0:T(8,128)S(1)} %copy-done.5, f32[512,1024]{1,0:T(8,128)S(1)} %get-tuple-element.14), kind=kOutput, calls=%fused_computation.11 | convolution fusion | flops 6443499520 | bytes 12582912 | tf_op jit(solution)/shard_map/dot_general | solution.py:29
  396.3 0.0 copy-done.4
  396.3 0.0 copy-start.3
  396.3 10.1 %fusion.4 = f32[8192,1024]{1,0:T(8,128)} fusion(f32[8192,1024]{1,0:T(8,128)} %fusion.5, f32[512,1024]{1,0:T(8,128)S(1)} %copy-done.4, f32[512,1024]{1,0:T(8,128)S(1)} %get-tuple-element.14), kind=kOutput, calls=%fused_computation.9 | convolution fusion | flops 6443499520 | bytes 12582912 | tf_op jit(solution)/shard_map/dot_general | solution.py:29
  406.4 0.0 copy-done.3
  406.4 0.0 copy-start.2
  406.4 10.1 %fusion.3 = f32[8192,1024]{1,0:T(8,128)} fusion(f32[8192,1024]{1,0:T(8,128)} %fusion.4, f32[512,1024]{1,0:T(8,128)S(1)} %copy-done.3, f32[512,1024]{1,0:T(8,128)S(1)} %get-tuple-element.14), kind=kOutput, calls=%fused_computation.7 | convolution fusion | flops 6443499520 | bytes 12582912 | tf_op jit(solution)/shard_map/dot_general | solution.py:29
  416.5 0.0 copy-done.2
  416.5 0.0 copy-start.1
  416.5 10.3 %fusion.2 = f32[8192,1024]{1,0:T(8,128)} fusion(f32[8192,1024]{1,0:T(8,128)} %fusion.3, f32[512,1024]{1,0:T(8,128)S(1)} %copy-done.2, f32[512,1024]{1,0:T(8,128)S(1)} %get-tuple-element.14), kind=kOutput, calls=%fused_computation.5 | convolution fusion | flops 6443499520 | bytes 12582912 | tf_op jit(solution)/shard_map/dot_general | solution.py:29
  426.8 0.0 copy-done.1
  426.8 0.0 copy-start
  426.8 10.1 %fusion.1 = f32[8192,1024]{1,0:T(8,128)} fusion(f32[8192,1024]{1,0:T(8,128)} %fusion.2, f32[512,1024]{1,0:T(8,128)S(1)} %copy-done.1, f32[512,1024]{1,0:T(8,128)S(1)} %get-tuple-element.14), kind=kOutput, calls=%fused_computation.3 | convolution fusion | flops 6443499520 | bytes 12582912 | tf_op jit(solution)/shard_map/dot_general | solution.py:29
  436.9 0.0 copy-done
  436.9 9.9 %fusion = f32[8192,1024]{1,0:T(8,128)} fusion(f32[8192,1024]{1,0:T(8,128)} %fusion.1, f32[512,1024]{1,0:T(8,128)S(1)} %copy-done, f32[512,1024]{1,0:T(8,128)S(1)} %get-tuple-element.14), kind=kOutput, calls=%fused_computation.1 | convolution fusion | flops 6443499520 | bytes 12582912 | tf_op jit(solution)/shard_map/dot_general | solution.py:29
Async XLA Ops:
  6.5 23.5 %copy-start.7 = (f32[256,1024]{1,0:T(8,128)S(1)}, f32[256,1024]{1,0:T(8,128)}, u32[]{:S(2)}) copy-start(f32[256,1024]{1,0:T(8,128)} %param.2) | copy-start | bytes 3145732
  6.5 359.1 %all-reduce.3.cloned.1.call-start = ((), (), s32[]{:S(2)}) async-start(), calls=%async_computation | async-start | bytes 33554432 | tf_op jit(solution)/shard_map/psum | solution.py:9
  30.1 26.3 %collective-permute-start = (f32[256,1024]{1,0:T(8,128)S(1)}, f32[256,1024]{1,0:T(8,128)}, u32[]{:S(2)}, u32[]{:S(2)}) collective-permute-start(f32[256,1024]{1,0:T(8,128)S(1)} %copy-done.7), channel_id=1, source_target_pairs={{0,16},{16,0},{1,17},{17,1},{2,18},{18,2},{3,19},{19,3},{4,20},{20... | collective-permute-start | bytes 3145736 | tf_op jit(solution)/shard_map/ppermute | solution.py:17
  365.6 10.4 %copy-start.6 = (f32[512,1024]{1,0:T(8,128)S(1)}, f32[512,1024]{1,0:T(8,128)}, u32[]{:S(2)}) copy-start(f32[512,1024]{1,0:T(8,128)} %get-tuple-element.6) | copy-start | bytes 6291460
  376.0 10.1 %copy-start.5 = (f32[512,1024]{1,0:T(8,128)S(1)}, f32[512,1024]{1,0:T(8,128)}, u32[]{:S(2)}) copy-start(f32[512,1024]{1,0:T(8,128)} %get-tuple-element.7) | copy-start | bytes 6291460
  386.1 10.2 %copy-start.4 = (f32[512,1024]{1,0:T(8,128)S(1)}, f32[512,1024]{1,0:T(8,128)}, u32[]{:S(2)}) copy-start(f32[512,1024]{1,0:T(8,128)} %get-tuple-element.8) | copy-start | bytes 6291460
  396.3 10.1 %copy-start.3 = (f32[512,1024]{1,0:T(8,128)S(1)}, f32[512,1024]{1,0:T(8,128)}, u32[]{:S(2)}) copy-start(f32[512,1024]{1,0:T(8,128)} %get-tuple-element.9) | copy-start | bytes 6291460
  406.4 10.1 %copy-start.2 = (f32[512,1024]{1,0:T(8,128)S(1)}, f32[512,1024]{1,0:T(8,128)}, u32[]{:S(2)}) copy-start(f32[512,1024]{1,0:T(8,128)} %get-tuple-element.10) | copy-start | bytes 6291460
  416.5 10.3 %copy-start.1 = (f32[512,1024]{1,0:T(8,128)S(1)}, f32[512,1024]{1,0:T(8,128)}, u32[]{:S(2)}) copy-start(f32[512,1024]{1,0:T(8,128)} %get-tuple-element.11) | copy-start | bytes 6291460
  426.8 10.1 %copy-start = (f32[512,1024]{1,0:T(8,128)S(1)}, f32[512,1024]{1,0:T(8,128)}, u32[]{:S(2)}) copy-start(f32[512,1024]{1,0:T(8,128)} %get-tuple-element.12) | copy-start | bytes 6291460
Sparse Core Ops, SparseCore 0:
  65.8 299.7 all-reduce.2
